TPU v7x, 32 devices: a whole 2x2x4 slice. The times are simulated.
32 devices in a mesh: dp: 4 (over y, core), ctx: 4 (over z), tsp: 2 (over x).
Axes of the slice: x: 2, y: 2, z: 4, core: 2. Of those that a mesh axis runs over, the one named last changes fastest.
Arguments:
- grad_out: bfloat16 [4, 1024, 8192], P('dp', 'ctx', 'tsp'), may hold values from -6 to 6
- attn_out: bfloat16 [4, 1024, 4096], P('dp', None, 'ctx'), may hold values from -6 to 6
- out_weight: bfloat16 [4096, 8192], P('ctx', 'tsp'), may hold values from -0.0625 to 0.0625
- query: bfloat16 [4, 1024, 4096], P('dp', 'tsp', 'ctx'), may hold values from -128 to 128
- keys: bfloat16 [4, 1024, 512], P('dp'), may hold values from -128 to 128
- values: bfloat16 [4, 1024, 512], P('dp'), may hold values from -6 to 6
- segment_ids: int32 [4, 1024], P('dp'), may hold values from 0 to 7, never falling along the last dimension, each value on 1 to 256 neighbouring positions
- tile_live: int32 [4, 8, 8], P('dp'), may hold values 0 or 1
Outputs:
- grad_query: bfloat16 [4, 1024, 4096], P('dp', 'tsp', 'ctx')
- grad_keys: bfloat16 [4, 1024, 512], P('dp', ('ctx', 'tsp'))
- grad_values: bfloat16 [4, 1024, 512], P('dp', ('ctx', 'tsp'))
- grad_weight: float32 [4096, 8192], P('ctx', 'tsp')
Inputs may be any that keep to these rules, and one draw needn't show every extreme that they name: `segment_ids`: segment numbers never fall along a row and segment 0 is the source document; each segment has 1 to 256 tokens, one exactly that many.
All inputs are finite; a program needn't handle non-finite values. No bound on the sum of `tile_live` on one device may be relied on, other than what follows from the above.
Results may differ from a plain program's by a relative error of at most 0.0058.
Values may be sent and summed in bfloat16 or wider, within the bound.
A program may use at most 128 MiB of HBM per device.

v0:
```python
import math
import jax
import jax.numpy as jnp
from jax import lax
from jax.sharding import PartitionSpec as P

HEADS = 32
KV_HEADS = 4
HEAD_DIM = 128
TILE = 128


def merge_group(tensor_in):
    row_count = tensor_in.shape[0]
    folded = tensor_in.reshape(row_count, KV_HEADS, HEADS // KV_HEADS, HEAD_DIM).sum(axis=2)
    return folded.reshape(row_count, KV_HEADS * HEAD_DIM)


def per_device(grad_out, attn_out, out_weight, query, keys, values, segment_ids, tile_live):
    score_scale = 1.0 / math.sqrt(HEAD_DIM)
    out_all = attn_out[0]
    seq_len = out_all.shape[0]
    feat_width = out_all.shape[1]
    dy_block = lax.all_gather(grad_out, "ctx", axis=1, tiled=True)[0]
    proj_rows = lax.dot_general(
        dy_block, out_weight, (((1,), (1,)), ((), ())), preferred_element_type=jnp.float32
    )
    grad_part = proj_rows
    weight_part = lax.dot_general(
        out_all, dy_block, (((0,), (0,)), ((), ())), preferred_element_type=jnp.float32
    )
    grad_part, weight_part = (grad_part, weight_part)
    weight_quarter = lax.psum_scatter(
        weight_part.astype(jnp.bfloat16), "dp", scatter_dimension=0, tiled=True
    )
    grad_weight = lax.all_gather(weight_quarter, "dp", axis=0, tiled=True).astype(jnp.float32)
    out_grad = lax.psum_scatter(grad_part, "tsp", scatter_dimension=0, tiled=True).astype(
        jnp.bfloat16
    )
    quarter = out_grad.shape[0]
    row_start = lax.axis_index("tsp") * quarter
    heads_dev = feat_width // HEAD_DIM
    group_size = HEADS // KV_HEADS
    head_ids = lax.axis_index("ctx") * heads_dev + jnp.arange(heads_dev, dtype=jnp.int32)
    kv_ids = head_ids // group_size
    query_pos = row_start + jnp.arange(quarter, dtype=jnp.int32)
    key_pos = jnp.arange(seq_len, dtype=jnp.int32)
    tile_count = seq_len // TILE
    tile_rows = lax.dynamic_slice_in_dim(tile_live[0], row_start // TILE, quarter // TILE, 0)
    tile_mask = (
        jnp.broadcast_to(
            tile_rows[:, None, :, None], (quarter // TILE, TILE, tile_count, TILE)
        ).reshape(quarter, seq_len)
        == 1
    )
    same_tile = query_pos[:, None] // TILE == key_pos[None, :] // TILE
    segments = segment_ids[0]
    query_seg = lax.dynamic_slice_in_dim(segments, row_start, quarter, 0)
    same_doc = (segments[None, :] == query_seg[:, None]) | (segments[None, :] == 0)
    allowed = (tile_mask | same_tile) & same_doc & (key_pos[None, :] <= query_pos[:, None])
    query_heads = query[0].reshape(quarter, heads_dev, HEAD_DIM)
    grad_heads = out_grad.reshape(quarter, heads_dev, HEAD_DIM)
    output_heads = lax.dynamic_slice_in_dim(out_all, row_start, quarter, 0).reshape(
        quarter, heads_dev, HEAD_DIM
    )
    key_heads = jnp.take(keys[0].reshape(seq_len, KV_HEADS, HEAD_DIM), kv_ids, axis=1)
    value_heads = jnp.take(values[0].reshape(seq_len, KV_HEADS, HEAD_DIM), kv_ids, axis=1)
    scores = (
        jnp.einsum("qhd,khd->hqk", query_heads, key_heads, preferred_element_type=jnp.float32)
        * score_scale
    )
    scores = jnp.where(allowed[None], scores, -jnp.inf)
    row_max = jnp.max(scores, axis=2, keepdims=True)
    lse = row_max + jnp.log(jnp.sum(jnp.exp(scores - row_max), axis=2, keepdims=True))
    probs_f = jnp.where(allowed[None], jnp.exp(scores - lse), 0.0)
    probs = probs_f.astype(jnp.bfloat16)
    value_terms = jnp.einsum("hqk,qhd->hkd", probs, grad_heads, preferred_element_type=jnp.float32)
    dprobs = jnp.einsum("qhd,khd->hqk", grad_heads, value_heads, preferred_element_type=jnp.float32)
    delta = jnp.sum(grad_heads.astype(jnp.float32) * output_heads.astype(jnp.float32), axis=2).T[
        :, :, None
    ]
    dscores = (probs_f * (dprobs - delta)).astype(jnp.bfloat16)
    grad_query = (
        (
            jnp.einsum("hqk,khd->qhd", dscores, key_heads, preferred_element_type=jnp.float32)
            * score_scale
        )
        .astype(jnp.bfloat16)
        .reshape(quarter, feat_width)
    )
    key_terms = (
        jnp.einsum("hqk,qhd->hkd", dscores, query_heads, preferred_element_type=jnp.float32)
        * score_scale
    )
    local_groups = max(1, heads_dev // group_size)

    def fold_local(terms):
        folded = terms.reshape(local_groups, heads_dev // local_groups, seq_len, HEAD_DIM).sum(
            axis=1
        )
        return folded.transpose(1, 0, 2).reshape(seq_len, local_groups * HEAD_DIM)

    def fold_remote(recv):
        spread = recv.shape[1] // (KV_HEADS * HEAD_DIM)
        folded = recv.reshape(recv.shape[0], KV_HEADS, spread, HEAD_DIM).sum(axis=2)
        return folded.reshape(recv.shape[0], KV_HEADS * HEAD_DIM)

    key_recv = lax.all_to_all(fold_local(key_terms), "ctx", split_axis=0, concat_axis=1, tiled=True)
    value_recv = lax.all_to_all(
        fold_local(value_terms), "ctx", split_axis=0, concat_axis=1, tiled=True
    )
    key_part = lax.psum_scatter(fold_remote(key_recv), "tsp", scatter_dimension=0, tiled=True)
    value_part = lax.psum_scatter(fold_remote(value_recv), "tsp", scatter_dimension=0, tiled=True)
    grad_keys = key_part.astype(jnp.bfloat16)[None]
    grad_values = value_part.astype(jnp.bfloat16)[None]
    return (grad_query[None], grad_keys, grad_values, grad_weight)


def solution(mesh):
    placed = (
        P("dp", "ctx", "tsp"),
        P("dp", None, "ctx"),
        P("ctx", "tsp"),
        P("dp", "tsp", "ctx"),
        P("dp", None, None),
        P("dp", None, None),
        P("dp", None),
        P("dp", None, None),
    )
    return jax.shard_map(
        per_device,
        mesh=mesh,
        in_specs=placed,
        out_specs=(
            P("dp", "tsp", "ctx"),
            P("dp", ("ctx", "tsp"), None),
            P("dp", ("ctx", "tsp"), None),
            P("ctx", "tsp"),
        ),
        check_vma=False,
    )
```

profile of v0, /device:TPU:0, one launch (start us, length us, event | category | flops | bytes accessed | tf_op | source)
XLA Modules:
  0.0 416.2 jit_solution(13732216424792096202)
XLA Ops:
  7.2 0.7 all-gather.3.cloned.1.call-update
  8.0 154.0 %all-gather.3.cloned.1.call-done = bf16[1,1024,4096]{2,1,0:T(8,128)(2,1)} async-done(((bf16[1,256,4096]{2,1,0:T(8,128)(2,1)}), bf16[1,1024,4096]{2,1,0:T(8,128)(2,1)}) %all-gather.3.cloned.1.call-update) | async-done | bytes 8388624 | tf_op jit(solution)/shard_map/all_gather | solution.py:24
  161.9 15.1 %fusion.6 = f32[1024,1024]{1,0:T(8,128)} fusion(bf16[1024,4096]{1,0:T(8,128)(2,1)} %param.12, bf16[1,1024,4096]{2,1,0:T(8,128)(2,1)} %all-gather.3.cloned.1.call-done), kind=kOutput, calls=%fused_computation.12 | convolution fusion | flops 8589934592 | bytes 20971520 | tf_op jit(solution)/shard_map/dot_general | solution.py:25
  177.0 0.2 reduce-scatter.11.cloned.1.call-start
  177.2 14.6 %fusion.8 = bf16[1024,4096]{1,0:T(8,128)(2,1)} fusion(bf16[1,1024,4096]{2,1,0:T(8,128)(2,1)} %all-gather.3.cloned.1.call-done, bf16[1,1024,1024]{2,1,0:T(8,128)(2,1)S(1)} %copy-done.9), kind=kOutput, calls=%fused_computation.14 | convolution fusion | flops 8594128896 | bytes 18874368 | tf_op jit(solution)/shard_map/dot_general | solution.py:29
  191.9 0.6 copy-done.11
  192.5 0.1 copy.53
  192.6 0.4 copy-done.5
  193.1 1.2 copy.77
  194.3 0.5 copy.51
  194.8 0.7 copy.52
  195.5 1.6 convert_bitcast_fusion
  197.1 1.8 copy.79
  198.9 1.5 copy.55
  200.4 0.7 copy.56
  201.1 2.2 gather_fusion
  203.3 2.2 gather_fusion.1
  205.6 0.3 broadcast_in_dim.59
  205.9 1.5 fusion.19
  207.5 9.4 %fusion.3 = (f32[8,512]{1,0:T(8,128)S(1)}, f32[8,1024,512]{2,1,0:T(8,128)}) fusion(pred[512,1024]{0,1:T(8,128)(4,1)S(1)} %fusion.19, bf16[512,8,128]{2,1,0:T(8,128)(2,1)S(1)} %bitcast.109, bf16[8,1024,128]{2,1,0:T(8,128)(2,1)} %gather_fusion, pred[8]{0:T(512)(128)(4,1)S(1)} %compare_and_fusion), kind=kOutput, calls=%fused_computation.9 | convolution fusion | flops 1087369216 | bytes 20463624 | tf_op jit(solution)/shard_map/qhd,khd->hqk/dot_general | solution.py:69
  216.9 9.4 %exponential_reduce_fusion = f32[8,512]{1,0:T(8,128)S(1)} fusion(f32[8,1024,512]{2,1,0:T(8,128)} %get-tuple-element.24, f32[8,512]{1,0:T(8,128)S(1)} %get-tuple-element.23, pred[512,1024]{0,1:T(8,128)(4,1)S(1)} %fusion.19), kind=kLoop, calls=%fused_computation.8 | loop fusion | flops 16773120 | bytes 17334272 | tf_op jit(solution)/shard_map/reduce_sum | solution.py:74
  226.3 1.5 fusion.43
  227.9 1.9 reduce-scatter.5.cloned.1.call-done
  229.7 2.9 convert_bitcast_fusion.1
  232.6 0.3 copy.78
  232.9 0.7 multiply_reduce_fusion.1
  233.6 0.4 copy-done.1
  234.1 11.7 %multiply_convert_fusion = bf16[8,512,1024]{1,2,0:T(8,128)(2,1)S(1)} fusion(f32[8,1024,512]{2,1,0:T(8,128)} %get-tuple-element.24, f32[8,512]{1,0:T(8,128)S(1)} %copy.58, f32[8,512]{1,0:T(8,128)S(1)} %log_add_fusion, pred[512,1024]{0,1:T(8,128)(4,1)S(1)} %copy-done.4, bf16[8,1024,128]{2,1,0:T(8,128)(2,1)} %gather_fusion.1, ...), kind=kOutput, calls=%fused_computation.7 | convolution fusion | flops 1104150528 | bytes 28868616 | tf_op jit(solution)/shard_map/qhd,khd->hqk/dot_general | solution.py:78
  245.8 3.5 multiply_reduce_fusion
  249.3 4.3 %all-to-all-start = ((f32[4,256,128]{2,1,0:T(8,128)}), f32[4,256,128]{2,1,0:T(8,128)S(1)}, u32[]{:S(2)}, u32[]{:S(2)}) async-start(f32[4,256,128]{2,1,0:T(8,128)} %bitcast.12), calls=%async_computation.1 | async-start | bytes 1048576 | tf_op jit(solution)/shard_map/all_to_all | solution.py:108
  253.7 11.3 %fusion.2 = bf16[1024,512,8]{1,0,2:T(8,128)(2,1)} fusion(f32[8,1024,512]{2,1,0:T(8,128)} %get-tuple-element.24, f32[512,8]{0,1:T(8,128)S(1)} %bitcast.113, pred[1024,512]{1,0:T(8,128)(4,1)S(1)} %fusion.43), kind=kLoop, calls=%fused_computation.5 | loop fusion | flops 20971520 | bytes 25706496 | tf_op jit(solution)/shard_map/convert_element_type | solution.py:76
  265.0 3.0 all-to-all-done
  268.0 1.0 copy.63
  269.0 0.3 reduce-scatter.9.cloned.1.call-start
  269.4 6.0 %convolution_bitcast_fusion = f32[4,256,128]{2,1,0:T(8,128)S(1)} fusion(bf16[4,256,512,8]{2,1,0,3:T(8,128)(2,1)} %bitcast.97, bf16[512,8,128,1]{2,1,0,3:T(8,128)(2,1)S(1)} %bitcast.101), kind=kOutput, calls=%fused_computation.32 | convolution fusion | flops 1073741824 | bytes 9961472 | tf_op jit(solution)/shard_map/hqk,qhd->hkd/dot_general | solution.py:77
  275.3 16.5 %all_to_all.29 = f32[4,256,128]{2,1,0:T(8,128)S(1)} all-to-all(f32[4,256,128]{2,1,0:T(8,128)S(1)} %convolution_bitcast_fusion), channel_id=1, replica_groups=mesh['dp'=4,'ctx'=4,'tsp'=2] {'ctx'}, dimensions={0} | all-to-all | bytes 1048576 | tf_op jit(solution)/shard_map/all_to_all | solution.py:109
  291.8 1.0 copy.65
  292.9 10.9 %reduce-scatter.11.cloned.1.call-done = bf16[256,4096]{1,0:T(8,128)(2,1)} async-done(((bf16[1024,4096]{1,0:T(8,128)(2,1)}), bf16[256,4096]{1,0:T(8,128)(2,1)}) %reduce-scatter.11.cloned.1.call-update) | async-done | bytes 2097168 | tf_op jit(solution)/shard_map/reduce_scatter | solution.py:33
  303.8 5.6 %multiply_convert_fusion.1 = bf16[8,128,512]{2,1,0:T(8,128)(2,1)S(1)} fusion(bf16[8,512,1024]{1,2,0:T(8,128)(2,1)} %copy-done.12, bf16[8,1024,128]{2,1,0:T(8,128)(2,1)} %gather_fusion, pred[8]{0:T(512)(128)(4,1)S(1)} %compare_and_fusion), kind=kOutput, calls=%fused_computation.24 | convolution fusion | flops 1075838976 | bytes 11534344 | tf_op jit(solution)/shard_map/hqk,khd->qhd/dot_general | solution.py:85
  309.4 1.3 copy.66
  310.7 10.3 %reduce-scatter.7.cloned.1.call-done = f32[128,512]{0,1:T(8,128)} async-done(((f32[256,512]{0,1:T(8,128)}), f32[128,512]{0,1:T(8,128)}) %reduce-scatter.7.cloned.1.call-update) | async-done | bytes 262160 | tf_op jit(solution)/shard_map/reduce_scatter | solution.py:112
  321.1 1.0 convert_bitcast_fusion.4
  322.0 0.8 copy.67
  322.8 15.0 %reduce-scatter.9.cloned.1.call-done = f32[128,512]{0,1:T(8,128)} async-done(((f32[256,512]{0,1:T(8,128)}), f32[128,512]{0,1:T(8,128)}) %reduce-scatter.9.cloned.1.call-update) | async-done | bytes 262160 | tf_op jit(solution)/shard_map/reduce_scatter | solution.py:113
  337.8 1.0 convert_bitcast_fusion.3
  338.8 0.8 copy.68
  339.5 58.0 %all-gather.5.cloned.1.call-done = bf16[1024,4096]{1,0:T(8,128)(2,1)} async-done(((bf16[256,4096]{1,0:T(8,128)(2,1)}), bf16[1024,4096]{1,0:T(8,128)(2,1)}) %all-gather.5.cloned.1.call-update) | async-done | bytes 8388624 | tf_op jit(solution)/shard_map/all_gather | solution.py:36
  397.5 11.8 %convert_element_type.48 = f32[1024,4096]{1,0:T(8,128)} convert(bf16[1024,4096]{1,0:T(8,128)(2,1)} %all-gather.5.cloned.1.call-done) | non-fusion elementwise | flops 4194304 | bytes 25165824 | tf_op jit(solution)/shard_map/convert_element_type | solution.py:36
  (42 shorter events, 0.4 us)
Async XLA Ops:
  7.2 154.7 %all-gather.3.cloned.1.call-start = ((), (), s32[]{:S(2)}) async-start(), calls=%async_computation.6 | async-start | bytes 10485760 | tf_op jit(solution)/shard_map/all_gather | solution.py:24
  7.9 169.3 %copy-start.9 = (bf16[1,1024,1024]{2,1,0:T(8,128)(2,1)S(1)}, bf16[1,1024,1024]{2,1,0:T(8,128)(2,1)}, u32[]{:S(2)}) copy-start(bf16[1,1024,1024]{2,1,0:T(8,128)(2,1)} %param.11) | copy-start | bytes 6291460
  7.9 221.8 %reduce-scatter.5.cloned.1.call-start = ((), (), s32[]{:S(2)}) async-start(), calls=%async_computation.7 | async-start | bytes 6291456 | tf_op jit(solution)/shard_map/reduce_scatter | solution.py:37
  177.0 126.7 %reduce-scatter.11.cloned.1.call-start = ((), (), s32[]{:S(2)}) async-start(), calls=%async_computation.10 | async-start | bytes 10485760 | tf_op jit(solution)/shard_map/reduce_scatter | solution.py:33
  191.8 0.7 copy-start.11
  191.8 1.2 copy-start.5
  191.8 2.5 copy-start.6
  197.1 8.4 %copy-start.10 = (s32[1,1024]{1,0:T(1,128)S(1)}, s32[1,1024]{1,0:T(1,128)}, u32[]{:S(2)}) copy-start(s32[1,1024]{1,0:T(1,128)} %param.16) | copy-start | bytes 12292
  201.1 6.4 %copy-start.7 = (bf16[64,8,8,128]{3,2,1,0:T(8,128)(2,1)S(1)}, bf16[64,8,8,128]{3,2,1,0:T(8,128)(2,1)}, u32[]{:S(2)}) copy-start(bf16[64,8,8,128]{3,2,1,0:T(8,128)(2,1)} %copy.77) | copy-start | bytes 3145732
  207.4 9.4 %copy-start.3 = (pred[512,1024]{0,1:T(8,128)(4,1)}, pred[512,1024]{0,1:T(8,128)(4,1)S(1)}, u32[]{:S(2)}) copy-start(pred[512,1024]{0,1:T(8,128)(4,1)S(1)} %fusion.19) | copy-start | bytes 1572868
  216.9 16.0 %copy-start = (f32[64,8,8,128]{3,2,1,0:T(8,128)S(1)}, f32[64,8,8,128]{3,2,1,0:T(8,128)}, u32[]{:S(2)}) copy-start(f32[64,8,8,128]{3,2,1,0:T(8,128)} %copy.79) | copy-start | bytes 6291460
  227.9 6.2 %copy-start.4 = (pred[512,1024]{0,1:T(8,128)(4,1)S(1)}, pred[512,1024]{0,1:T(8,128)(4,1)}, u32[]{:S(2)}) copy-start(pred[512,1024]{0,1:T(8,128)(4,1)} %copy-done.3) | copy-start | bytes 1572868
  232.9 1.0 copy-start.1
  234.0 11.7 %copy-start.8 = (bf16[64,8,8,128]{3,2,1,0:T(8,128)(2,1)S(1)}, bf16[64,8,8,128]{3,2,1,0:T(8,128)(2,1)}, u32[]{:S(2)}) copy-start(bf16[64,8,8,128]{3,2,1,0:T(8,128)(2,1)} %copy.77) | copy-start | bytes 3145732
  245.8 3.6 copy-start.12
  249.3 18.7 %all-to-all-start = ((f32[4,256,128]{2,1,0:T(8,128)}), f32[4,256,128]{2,1,0:T(8,128)S(1)}, u32[]{:S(2)}, u32[]{:S(2)}) async-start(f32[4,256,128]{2,1,0:T(8,128)} %bitcast.12), calls=%async_computation.1 | async-start | bytes 1048576 | tf_op jit(solution)/shard_map/all_to_all | solution.py:108
  253.7 67.4 %reduce-scatter.7.cloned.1.call-start = ((), (), s32[]{:S(2)}) async-start(), calls=%async_computation.8 | async-start | bytes 786432 | tf_op jit(solution)/shard_map/reduce_scatter | solution.py:112
  253.7 15.7 %copy-start.2 = (bf16[64,8,8,128]{3,2,1,0:T(8,128)(2,1)S(1)}, bf16[64,8,8,128]{3,2,1,0:T(8,128)(2,1)}, u32[]{:S(2)}) copy-start(bf16[64,8,8,128]{3,2,1,0:T(8,128)(2,1)} %copy-done.1) | copy-start | bytes 3145732
  269.0 68.8 %reduce-scatter.9.cloned.1.call-start = ((), (), s32[]{:S(2)}) async-start(), calls=%async_computation.9 | async-start | bytes 786432 | tf_op jit(solution)/shard_map/reduce_scatter | solution.py:113
  292.8 104.7 %all-gather.5.cloned.1.call-start = ((), (), s32[]{:S(2)}) async-start(), calls=%async_computation.11 | async-start | bytes 10485760 | tf_op jit(solution)/shard_map/all_gather | solution.py:36
Sparse Core Ops, SparseCore 0:
  9.5 152.3 all-gather.2
  177.1 52.5 reduce-scatter.4
  232.3 71.3 reduce-scatter.10
  306.4 14.6 reduce-scatter.6
  323.1 14.6 reduce-scatter.8
  339.2 58.2 all-gather.4
where the time goes:
time: 417 us; the launch traced here: 416 us
  waiting for transfers between devices  254 us (61%)
  matrix products  65.9 us (16%)
  other arithmetic  42.8 us (10%)
  local copies, waits for them, and re-layouts  17.9 us (4%)
  blocking collectives  16.5 us (4%)
  between operations  14.4 us (3%)
  starting transfers between devices  4.98 us (1%)
    all_gather x1, waiting for transfers between devices, per_device(): dy_block = lax.all_gather(grad_out, 'ctx', axis=1, tiled=True)[0]  154 us
    all_gather x1, waiting for transfers between devices, per_device(): lax.all_gather(weight_quarter, 'dp', axis=0, tiled=True).astype(jnp.float32)  58 us
    all_to_all x1, blocking collectives, per_device(): lax.all_to_all(fold_local(value_terms), 'ctx', split_axis=0, concat_axis=...  16.5 us
    dot_general x1, matrix products, per_device(): lax.dot_general(dy_block, out_weight, (((1,), (1,)), ((), ())), preferred...  15.1 us
    reduce_scatter x1, waiting for transfers between devices, per_device(): lax.psum_scatter(fold_remote(value_recv), 'tsp', scatter_dimension=0, til...  15 us
    dot_general x1, matrix products, per_device(): lax.dot_general(out_all, dy_block, (((0,), (0,)), ((), ())), preferred_el...  14.6 us
    convert_element_type x1, other arithmetic, per_device(): lax.all_gather(weight_quarter, 'dp', axis=0, tiled=True).astype(jnp.float32)  11.8 us
    dot_general x1, matrix products, per_device(): jnp.einsum('qhd,khd->hqk', grad_heads, value_heads, preferred_element_typ...  11.7 us
  transfers between devices with their start and end apart: 7, of which 7 were waited for; matrix products, arithmetic and copies ran while one was open for 24% of the time, Pallas kernels for 0%

commit v1 on v0

--- a/solution.py
+++ b/solution.py
@@ -8,6 +8,14 @@
 KV_HEADS = 4
 HEAD_DIM = 128
 TILE = 128
+
+
+def end_tokens(x_local):
+    answer = lax.axis_size("ctx")
+    opened = jnp.split(x_local, answer, 0)
+    piece_next = jnp.stack(opened, 0)
+    wide_out = lax.all_to_all(piece_next, "ctx", 0, 0)
+    return jnp.concatenate(wide_out, 1)
 
 
 def merge_group(tensor_in):
@@ -106,9 +114,7 @@
         return folded.reshape(recv.shape[0], KV_HEADS * HEAD_DIM)
 
     key_recv = lax.all_to_all(fold_local(key_terms), "ctx", split_axis=0, concat_axis=1, tiled=True)
-    value_recv = lax.all_to_all(
-        fold_local(value_terms), "ctx", split_axis=0, concat_axis=1, tiled=True
-    )
+    value_recv = end_tokens(fold_local(value_terms))
     key_part = lax.psum_scatter(fold_remote(key_recv), "tsp", scatter_dimension=0, tiled=True)
     value_part = lax.psum_scatter(fold_remote(value_recv), "tsp", scatter_dimension=0, tiled=True)
     grad_keys = key_part.astype(jnp.bfloat16)[None]

time: 417 us -> 417 us (level)
  other arithmetic: 42.8 us -> 30 us
  waiting for transfers between devices: 254 us -> 265 us
    convert_element_type x1 -> x0, other arithmetic: 11.3 us -> none  [per_device(): probs = probs_f.astype(jnp.bfloat16)]
    reduce_scatter x1, waiting for transfers between devices: 10.9 us -> 17.3 us  [per_device(): lax.psum_scatter(weight_part.astype(jnp.bfloat16), 'dp', scatter_dimensio...]
    unnamed x34 -> x30, local copies, waits for them, and re-layouts: 9.7 us -> 9.51 us
  transfers between devices with their start and end apart: 7 -> 7, of which waited for: 7 -> 7; matrix products, arithmetic and copies ran while one was open for 24% -> 21% of each run, Pallas kernels for 0% -> 0%
where the time goes in v1:
time: 417 us; the launch traced here: 416 us
  waiting for transfers between devices  265 us (64%)
  matrix products  67.2 us (16%)
  other arithmetic  30 us (7%)
  local copies, waits for them, and re-layouts  17.7 us (4%)
  blocking collectives  16.4 us (4%)
  between operations  14.4 us (3%)
  starting transfers between devices  5.14 us (1%)
    all_gather x1, waiting for transfers between devices, per_device(): dy_block = lax.all_gather(grad_out, 'ctx', axis=1, tiled=True)[0]  154 us
    all_gather x1, waiting for transfers between devices, per_device(): lax.all_gather(weight_quarter, 'dp', axis=0, tiled=True).astype(jnp.float32)  58 us
    reduce_scatter x1, waiting for transfers between devices, per_device(): lax.psum_scatter(weight_part.astype(jnp.bfloat16), 'dp', scatter_dimensio...  17.3 us
    all_to_all x1, blocking collectives, end_tokens(): wide_out = lax.all_to_all(piece_next, 'ctx', 0, 0)  16.4 us
    dot_general x1, matrix products, per_device(): lax.dot_general(dy_block, out_weight, (((1,), (1,)), ((), ())), preferred...  15.1 us
    reduce_scatter x1, waiting for transfers between devices, per_device(): lax.psum_scatter(fold_remote(value_recv), 'tsp', scatter_dimension=0, til...  15 us
    dot_general x1, matrix products, per_device(): lax.dot_general(out_all, dy_block, (((0,), (0,)), ((), ())), preferred_el...  14.6 us
    convert_element_type x1, other arithmetic, per_device(): lax.all_gather(weight_quarter, 'dp', axis=0, tiled=True).astype(jnp.float32)  11.8 us
  transfers between devices with their start and end apart: 7, of which 7 were waited for; matrix products, arithmetic and copies ran while one was open for 21% of the time, Pallas kernels for 0%

profile of v1, /device:TPU:0, one launch (start us, length us, event | category | flops | bytes accessed | tf_op | source)
XLA Modules:
  0.0 416.2 jit_solution(12407456058514520362)
XLA Ops:
  7.2 0.7 all-gather.3.cloned.1.call-update
  8.0 154.0 %all-gather.3.cloned.1.call-done = bf16[1,1024,4096]{2,1,0:T(8,128)(2,1)} async-done(((bf16[1,256,4096]{2,1,0:T(8,128)(2,1)}), bf16[1,1024,4096]{2,1,0:T(8,128)(2,1)}) %all-gather.3.cloned.1.call-update) | async-done | bytes 8388624 | tf_op jit(solution)/shard_map/all_gather | solution.py:32
  161.9 15.1 %fusion.4 = f32[1024,1024]{1,0:T(8,128)} fusion(bf16[1024,4096]{1,0:T(8,128)(2,1)} %param.12, bf16[1,1024,4096]{2,1,0:T(8,128)(2,1)} %all-gather.3.cloned.1.call-done), kind=kOutput, calls=%fused_computation.10 | convolution fusion | flops 8589934592 | bytes 20971520 | tf_op jit(solution)/shard_map/dot_general | solution.py:33
  177.0 0.2 reduce-scatter.11.cloned.1.call-start
  177.2 14.6 %fusion.9 = bf16[1024,4096]{1,0:T(8,128)(2,1)} fusion(bf16[1,1024,4096]{2,1,0:T(8,128)(2,1)} %all-gather.3.cloned.1.call-done, bf16[1,1024,1024]{2,1,0:T(8,128)(2,1)S(1)} %copy-done.7), kind=kOutput, calls=%fused_computation.14 | convolution fusion | flops 8594128896 | bytes 18874368 | tf_op jit(solution)/shard_map/dot_general | solution.py:37
  191.9 0.6 copy-done.9
  192.5 0.1 copy.51
  192.6 0.4 copy-done.2
  193.1 1.2 copy.72
  194.3 0.5 copy.49
  194.8 0.7 copy.50
  195.5 1.6 convert_bitcast_fusion
  197.1 1.8 copy.74
  199.0 1.5 copy.53
  200.4 0.7 copy.54
  201.2 2.2 gather_fusion
  203.3 2.1 gather_fusion.1
  205.6 0.3 broadcast_in_dim.49
  205.9 1.5 fusion.20
  207.5 9.2 %fusion.1 = (f32[8,512]{1,0:T(8,128)S(1)}, f32[8,1024,512]{2,1,0:T(8,128)}) fusion(pred[512,1024]{0,1:T(8,128)(4,1)S(1)} %fusion.20, bf16[512,8,128]{2,1,0:T(8,128)(2,1)S(1)} %bitcast.97, bf16[8,1024,128]{2,1,0:T(8,128)(2,1)} %gather_fusion, pred[8]{0:T(512)(128)(4,1)S(1)} %compare_and_fusion), kind=kOutput, calls=%fused_computation.7 | convolution fusion | flops 1087369216 | bytes 20463624 | tf_op jit(solution)/shard_map/qhd,khd->hqk/dot_general | solution.py:77
  216.7 9.4 %exponential_reduce_fusion = f32[8,512]{1,0:T(8,128)S(1)} fusion(f32[8,1024,512]{2,1,0:T(8,128)} %get-tuple-element.28, f32[8,512]{1,0:T(8,128)S(1)} %get-tuple-element.27, pred[512,1024]{0,1:T(8,128)(4,1)S(1)} %fusion.20), kind=kLoop, calls=%fused_computation.5 | loop fusion | flops 16773120 | bytes 17334272 | tf_op jit(solution)/shard_map/reduce_sum | solution.py:82
  226.1 3.6 reduce-scatter.5.cloned.1.call-done
  229.7 2.9 convert_bitcast_fusion.1
  232.6 0.3 copy.73
  232.9 0.7 multiply_reduce_fusion.1
  233.6 0.1 copy.56
  233.7 11.3 %multiply_convert_fusion = bf16[8,512,1024]{1,2,0:T(8,128)(2,1)S(1)} fusion(f32[8,1024,512]{2,1,0:T(8,128)} %get-tuple-element.28, f32[8,512]{1,0:T(8,128)S(1)} %copy.56, f32[8,512]{1,0:T(8,128)S(1)} %log_add_fusion, pred[512,1024]{0,1:T(8,128)(4,1)S(1)} %fusion.20, bf16[8,1024,128]{2,1,0:T(8,128)(2,1)} %gather_fusion.1, ...), kind=kOutput, calls=%fused_computation.3 | convolution fusion | flops 1104150528 | bytes 28868616 | tf_op jit(solution)/shard_map/qhd,khd->hqk/dot_general | solution.py:86
  245.0 3.5 multiply_reduce_fusion
  248.6 0.2 copy-done.10
  248.7 4.5 %all-to-all-start = ((f32[4,256,128]{2,1,0:T(8,128)}), f32[4,256,128]{2,1,0:T(8,128)S(1)}, u32[]{:S(2)}, u32[]{:S(2)}) async-start(f32[4,256,128]{2,1,0:T(8,128)} %bitcast.12), calls=%async_computation.1 | async-start | bytes 1048576 | tf_op jit(solution)/shard_map/all_to_all | solution.py:116
  253.2 8.5 %fusion.24 = f32[1,1024,128]{2,1,0:T(8,128)S(1)} fusion(f32[8,1024,512]{2,1,0:T(8,128)} %get-tuple-element.28, f32[8,512]{1,0:T(8,128)S(1)} %log_add_fusion, pred[512,1024]{0,1:T(8,128)(4,1)S(1)} %fusion.20, bf16[64,8,8,128]{3,2,1,0:T(8,128)(2,1)S(1)} %copy-done.6), kind=kOutput, calls=%fused_computation.32 | convolution fusion | flops 1094713344 | bytes 18890752 | tf_op jit(solution)/shard_map/hqk,qhd->hkd/dot_general | solution.py:85
  261.7 5.8 %all-to-all-done = f32[4,256,128]{2,1,0:T(8,128)S(1)} async-done(((f32[4,256,128]{2,1,0:T(8,128)}), f32[4,256,128]{2,1,0:T(8,128)S(1)}, u32[]{:S(2)}, u32[]{:S(2)}) %all-to-all-start) | async-done | bytes 524320 | tf_op jit(solution)/shard_map/all_to_all | solution.py:116
  267.5 1.0 copy.61
  268.5 0.3 reduce-scatter.9.cloned.1.call-start
  268.9 16.4 %all_to_all.21 = f32[4,256,128]{2,1,0:T(8,128)S(1)} all-to-all(f32[4,256,128]{2,1,0:T(8,128)S(1)} %pad_maximum_fusion), channel_id=1, replica_groups=mesh['dp'=4,'ctx'=4,'tsp'=2] {'ctx'}, dimensions={0} | all-to-all | bytes 1048576 | tf_op jit(solution)/shard_map/all_to_all | solution.py:17
  285.4 1.0 copy.63
  286.4 0.0 all-gather.5.cloned.1.call-start
  286.5 17.3 %reduce-scatter.11.cloned.1.call-done = bf16[256,4096]{1,0:T(8,128)(2,1)} async-done(((bf16[1024,4096]{1,0:T(8,128)(2,1)}), bf16[256,4096]{1,0:T(8,128)(2,1)}) %reduce-scatter.11.cloned.1.call-update) | async-done | bytes 2097168 | tf_op jit(solution)/shard_map/reduce_scatter | solution.py:41
  303.8 5.0 %multiply_convert_fusion.1 = bf16[8,128,512]{2,1,0:T(8,128)(2,1)S(1)} fusion(bf16[8,512,1024]{1,2,0:T(8,128)(2,1)} %copy-done.10, bf16[8,1024,128]{2,1,0:T(8,128)(2,1)S(1)} %copy-done.1, pred[8]{0:T(512)(128)(4,1)S(1)} %compare_and_fusion), kind=kOutput, calls=%fused_computation.24 | convolution fusion | flops 1075838976 | bytes 11534344 | tf_op jit(solution)/shard_map/hqk,khd->qhd/dot_general | solution.py:93
  308.8 1.3 copy.64
  310.1 11.0 %reduce-scatter.7.cloned.1.call-done = f32[128,512]{0,1:T(8,128)} async-done(((f32[256,512]{0,1:T(8,128)}), f32[128,512]{0,1:T(8,128)}) %reduce-scatter.7.cloned.1.call-update) | async-done | bytes 262160 | tf_op jit(solution)/shard_map/reduce_scatter | solution.py:118
  321.1 1.0 convert_bitcast_fusion.4
  322.1 0.8 copy.65
  322.8 15.0 %reduce-scatter.9.cloned.1.call-done = f32[128,512]{0,1:T(8,128)} async-done(((f32[256,512]{0,1:T(8,128)}), f32[128,512]{0,1:T(8,128)}) %reduce-scatter.9.cloned.1.call-update) | async-done | bytes 262160 | tf_op jit(solution)/shard_map/reduce_scatter | solution.py:119
  337.8 1.0 convert_bitcast_fusion.3
  338.8 0.8 copy.66
  339.6 58.0 %all-gather.5.cloned.1.call-done = bf16[1024,4096]{1,0:T(8,128)(2,1)} async-done(((bf16[256,4096]{1,0:T(8,128)(2,1)}), bf16[1024,4096]{1,0:T(8,128)(2,1)}) %all-gather.5.cloned.1.call-update) | async-done | bytes 8388624 | tf_op jit(solution)/shard_map/all_gather | solution.py:44
  397.6 11.8 %convert_element_type.47 = f32[1024,4096]{1,0:T(8,128)} convert(bf16[1024,4096]{1,0:T(8,128)(2,1)} %all-gather.5.cloned.1.call-done) | non-fusion elementwise | flops 4194304 | bytes 25165824 | tf_op jit(solution)/shard_map/convert_element_type | solution.py:44
  (38 shorter events, 0.4 us)
Async XLA Ops:
  7.2 154.7 %all-gather.3.cloned.1.call-start = ((), (), s32[]{:S(2)}) async-start(), calls=%async_computation.6 | async-start | bytes 10485760 | tf_op jit(solution)/shard_map/all_gather | solution.py:32
  7.9 169.3 %copy-start.7 = (bf16[1,1024,1024]{2,1,0:T(8,128)(2,1)S(1)}, bf16[1,1024,1024]{2,1,0:T(8,128)(2,1)}, u32[]{:S(2)}) copy-start(bf16[1,1024,1024]{2,1,0:T(8,128)(2,1)} %param.11) | copy-start | bytes 6291460
  7.9 221.8 %reduce-scatter.5.cloned.1.call-start = ((), (), s32[]{:S(2)}) async-start(), calls=%async_computation.7 | async-start | bytes 6291456 | tf_op jit(solution)/shard_map/reduce_scatter | solution.py:45
  177.0 126.8 %reduce-scatter.11.cloned.1.call-start = ((), (), s32[]{:S(2)}) async-start(), calls=%async_computation.10 | async-start | bytes 10485760 | tf_op jit(solution)/shard_map/reduce_scatter | solution.py:41
  191.8 0.7 copy-start.9
  191.8 1.2 copy-start.2
  191.8 2.5 copy-start.3
  197.1 8.4 %copy-start.8 = (s32[1,1024]{1,0:T(1,128)S(1)}, s32[1,1024]{1,0:T(1,128)}, u32[]{:S(2)}) copy-start(s32[1,1024]{1,0:T(1,128)} %param.16) | copy-start | bytes 12292
  201.1 6.3 %copy-start.4 = (bf16[64,8,8,128]{3,2,1,0:T(8,128)(2,1)S(1)}, bf16[64,8,8,128]{3,2,1,0:T(8,128)(2,1)}, u32[]{:S(2)}) copy-start(bf16[64,8,8,128]{3,2,1,0:T(8,128)(2,1)} %copy.72) | copy-start | bytes 3145732
  216.7 16.2 %copy-start = (f32[64,8,8,128]{3,2,1,0:T(8,128)S(1)}, f32[64,8,8,128]{3,2,1,0:T(8,128)}, u32[]{:S(2)}) copy-start(f32[64,8,8,128]{3,2,1,0:T(8,128)} %copy.74) | copy-start | bytes 6291460
  233.7 11.3 %copy-start.5 = (bf16[64,8,8,128]{3,2,1,0:T(8,128)(2,1)S(1)}, bf16[64,8,8,128]{3,2,1,0:T(8,128)(2,1)}, u32[]{:S(2)}) copy-start(bf16[64,8,8,128]{3,2,1,0:T(8,128)(2,1)} %copy.72) | copy-start | bytes 3145732
  245.0 3.7 copy-start.10
  245.0 8.2 %copy-start.6 = (bf16[64,8,8,128]{3,2,1,0:T(8,128)(2,1)S(1)}, bf16[64,8,8,128]{3,2,1,0:T(8,128)(2,1)}, u32[]{:S(2)}) copy-start(bf16[64,8,8,128]{3,2,1,0:T(8,128)(2,1)} %get-tuple-element.21) | copy-start | bytes 3145732
  248.7 18.8 %all-to-all-start = ((f32[4,256,128]{2,1,0:T(8,128)}), f32[4,256,128]{2,1,0:T(8,128)S(1)}, u32[]{:S(2)}, u32[]{:S(2)}) async-start(f32[4,256,128]{2,1,0:T(8,128)} %bitcast.12), calls=%async_computation.1 | async-start | bytes 1048576 | tf_op jit(solution)/shard_map/all_to_all | solution.py:116
  253.2 67.9 %reduce-scatter.7.cloned.1.call-start = ((), (), s32[]{:S(2)}) async-start(), calls=%async_computation.8 | async-start | bytes 786432 | tf_op jit(solution)/shard_map/reduce_scatter | solution.py:118
  261.7 42.1 %copy-start.1 = (bf16[8,1024,128]{2,1,0:T(8,128)(2,1)S(1)}, bf16[8,1024,128]{2,1,0:T(8,128)(2,1)}, u32[]{:S(2)}) copy-start(bf16[8,1024,128]{2,1,0:T(8,128)(2,1)} %gather_fusion) | copy-start | bytes 6291460
  268.5 69.3 %reduce-scatter.9.cloned.1.call-start = ((), (), s32[]{:S(2)}) async-start(), calls=%async_computation.9 | async-start | bytes 786432 | tf_op jit(solution)/shard_map/reduce_scatter | solution.py:119
  286.4 111.1 %all-gather.5.cloned.1.call-start = ((), (), s32[]{:S(2)}) async-start(), calls=%async_computation.11 | async-start | bytes 10485760 | tf_op jit(solution)/shard_map/all_gather | solution.py:44
Sparse Core Ops, SparseCore 0:
  9.5 152.3 all-gather.2
  177.1 52.5 reduce-scatter.4
  232.3 71.4 reduce-scatter.10
  306.4 14.6 reduce-scatter.6
  323.2 14.6 reduce-scatter.8
  339.2 58.2 all-gather.4
